TPU v7x, 256 devices: a whole 4x4x8 slice. The times are simulated.
256 devices in a mesh: dp: 32 (over z, y), section: 2 (over core), tensor: 4 (over x).
Axes of the slice: x: 4, y: 4, z: 8, core: 2. Of those that a mesh axis runs over, the one named last changes fastest.
Arguments:
- tokens: bfloat16 [8192, 2048], P('dp'), may hold values from -6 to 6
- base_rows: int32 [128], replicated, may hold values from 1 to 6, as said below
- baseline_owner: int32 [128], replicated, may hold values from 0 to 31, as said below
- cotangent: bfloat16 [2, 16384, 2048], P('section', 'dp'), may hold values from -6 to 6
- pre_gain: float32 [2, 2048], P('section'), may hold values from 0.25 to 1.75
- input_proj: bfloat16 [2, 2048, 2048], P('section', None, 'tensor'), may hold values from -0.125 to 0.125
- gate_proj: bfloat16 [2, 2048, 2048], P('section', None, 'tensor'), may hold values from -0.125 to 0.125
- state_proj: bfloat16 [2, 2048, 256], P('section'), may hold values from -0.125 to 0.125
- step_proj: bfloat16 [2, 2048, 32], P('section', None, 'tensor'), may hold values from -0.125 to 0.125
- step_bias: float32 [2, 32], P('section', 'tensor'), may hold values from -6 to -1.5
- decay_log: float32 [2, 32], P('section', 'tensor'), may hold values from 0 to 2.5
- skip_gain: float32 [2, 32], P('section', 'tensor'), may hold values from 0.5 to 1.5
- norm_gain: float32 [2, 2048], P('section', 'tensor'), may hold values from 0.25 to 1.75
- out_proj: bfloat16 [2, 2048, 2048], P('section', 'tensor'), may hold values from -0.125 to 0.125
Outputs:
- activations: bfloat16 [2, 16384, 2048], P('section', 'dp')
- out_grad: bfloat16 [2, 2048, 2048], P('section', 'tensor', 'dp')
Inputs may be any that keep to these rules, and one draw needn't show every extreme that they name: `base_rows`: over all baselines they sum to 256; some baseline has exactly 6. `baseline_owner`: every owner holds exactly 4 baselines; the base_rows of one owner's baselines sum to at most 16, and for some owner to exactly 16.
All inputs are finite; a program needn't handle non-finite values.
Results may differ from a plain program's by a relative error of at most 0.025.
Values may be sent and summed in bfloat16 or wider, within the bound.
A program may use at most 128 MiB of HBM per device.

v0:
```python
import jax
import jax.numpy as jnp
from jax import lax
from jax.sharding import PartitionSpec as P

HEADS = 32
HEADDIM = 64
NSTATE = 128
BLOCK = 64
MICRO = 2
EPS = 1e-05


def from_behind(value, axis, steps):
    count = lax.axis_size(axis)
    first, last = (max(0, -steps), min(count, count - steps))
    return lax.ppermute(value, axis, [(source, source + steps) for source in range(first, last)])


def layout_tables(base_rows, baseline_owner):
    count = base_rows.shape[0]
    index = jnp.arange(count, dtype=jnp.int32)
    ends = jnp.cumsum(base_rows)
    starts = ends - base_rows
    earlier = (baseline_owner[:, None] == baseline_owner[None, :]) & (
        index[None, :] < index[:, None]
    )
    owner_start = jnp.sum(jnp.where(earlier, base_rows[None, :], 0), axis=1)
    return (index, starts, ends, owner_start)


def block_scan(
    heads_in, b_rows, c_rows, step_size, decay_rate, segment, state, prev_segment, block
):
    total_rows, head_count, head_dim = heads_in.shape
    blocks = total_rows // block

    def advance(carried_in, item):
        state_now, segment_before = carried_in
        x_blk, b_blk, c_blk, dt_blk, seg_blk = item
        running = jnp.cumsum(dt_blk * decay_rate[None, :], axis=0)
        positions = jnp.arange(block, dtype=jnp.int32)
        together = (seg_blk[:, None] == seg_blk[None, :]) & (
            positions[:, None] >= positions[None, :]
        )
        spread = jnp.minimum(running[:, None, :] - running[None, :, :], 0.0)
        decay_mask = jnp.where(together[:, :, None], jnp.exp(spread), 0.0)
        scores = jnp.dot(c_blk, b_blk.T, preferred_element_type=jnp.float32)
        weights = (decay_mask * scores[:, :, None] * dt_blk[None, :, :]).astype(jnp.bfloat16)
        within = jnp.einsum("ijh,jhp->ihp", weights, x_blk, preferred_element_type=jnp.float32)
        keep_in = (seg_blk == segment_before).astype(jnp.float32)
        readout = jnp.einsum(
            "in,hpn->ihp", c_blk, state_now.astype(jnp.bfloat16), preferred_element_type=jnp.float32
        )
        from_state = keep_in[:, None, None] * jnp.exp(running)[:, :, None] * readout
        last_segment = seg_blk[-1]
        tail_weight = (
            jnp.where(
                (seg_blk == last_segment)[:, None], jnp.exp(running[-1][None, :] - running), 0.0
            )
            * dt_blk
        )
        scaled = (tail_weight[:, :, None] * x_blk.astype(jnp.float32)).astype(jnp.bfloat16)
        fresh_term = jnp.einsum("jhp,jn->hpn", scaled, b_blk, preferred_element_type=jnp.float32)
        keep_state = (last_segment == segment_before).astype(jnp.float32)
        state_next = keep_state * jnp.exp(running[-1])[:, None, None] * state_now + fresh_term
        return ((state_next, last_segment), within + from_state)

    scanned = (
        heads_in.reshape(blocks, block, head_count, head_dim),
        b_rows.reshape(blocks, block, -1),
        c_rows.reshape(blocks, block, -1),
        step_size.reshape(blocks, block, head_count),
        segment.reshape(blocks, block),
    )
    (state, prev_segment), outputs = lax.scan(advance, (state, prev_segment), scanned)
    return (outputs.reshape(total_rows, head_count, head_dim), state, prev_segment)


def block_layer(rows_in, segment, carried_state, params):
    (
        pre_gain,
        input_proj,
        gate_proj,
        state_proj,
        step_proj,
        step_bias,
        decay_log,
        skip_gain,
        norm_gain,
        out_proj,
    ) = params
    row_count = rows_in.shape[0]
    local_heads = step_proj.shape[1]
    rows_f = rows_in.astype(jnp.float32)
    normed = (
        rows_f * lax.rsqrt(jnp.mean(rows_f * rows_f, axis=-1, keepdims=True) + EPS) * pre_gain
    ).astype(jnp.bfloat16)
    scan_in = jax.nn.silu(jnp.dot(normed, input_proj, preferred_element_type=jnp.float32)).astype(
        jnp.bfloat16
    )
    gate_pre = jnp.dot(normed, gate_proj, preferred_element_type=jnp.float32)
    state_io = jax.nn.silu(jnp.dot(normed, state_proj, preferred_element_type=jnp.float32)).astype(
        jnp.bfloat16
    )
    step_size = jax.nn.softplus(
        jnp.dot(normed, step_proj, preferred_element_type=jnp.float32) + step_bias
    )
    decay_rate = -jnp.exp(decay_log)
    heads_in = scan_in.reshape(row_count, local_heads, HEADDIM)
    scan_out, state_end, segment_end = block_scan(
        heads_in,
        state_io[:, :NSTATE],
        state_io[:, NSTATE:],
        step_size,
        decay_rate,
        segment,
        carried_state[0],
        carried_state[1],
        BLOCK,
    )
    scan_out = scan_out + skip_gain[None, :, None] * heads_in.astype(jnp.float32)
    gated = scan_out.reshape(row_count, local_heads * HEADDIM) * jax.nn.silu(gate_pre)
    sq_sum = lax.psum(jnp.sum(gated * gated, axis=-1), "tensor")
    y_norm = (gated * lax.rsqrt(sq_sum[:, None] / (HEADS * HEADDIM) + EPS) * norm_gain).astype(
        jnp.bfloat16
    )
    row_share = row_count // lax.axis_size("tensor")
    summed = lax.psum_scatter(
        jnp.dot(y_norm, out_proj, preferred_element_type=jnp.float32).astype(jnp.bfloat16),
        "tensor",
        scatter_dimension=0,
        tiled=True,
    ).astype(jnp.float32)
    own_rows = lax.dynamic_slice_in_dim(rows_f, lax.axis_index("tensor") * row_share, row_share, 0)
    own_out = (own_rows + summed).astype(jnp.bfloat16)
    result = lax.all_gather(own_out, "tensor", axis=0, tiled=True)
    return (result, y_norm, (state_end, segment_end))


def grad_term(y_norm, cot_rows):
    return lax.dot_general(
        y_norm, cot_rows, (((0,), (0,)), ((), ())), preferred_element_type=jnp.float32
    )


def per_device(
    tokens,
    base_rows,
    baseline_owner,
    cotangent,
    pre_gain,
    input_proj,
    gate_proj,
    state_proj,
    step_proj,
    step_bias,
    decay_log,
    skip_gain,
    norm_gain,
    out_proj,
):
    dp_count = lax.axis_size("dp")
    tok_rows, feat_width = tokens.shape
    slot_cap = 2 * tok_rows // dp_count
    own_slots = slot_cap * dp_count
    index, starts, ends, owner_start = layout_tables(base_rows, baseline_owner)
    local = jnp.arange(tok_rows, dtype=jnp.int32)
    inside = ((starts[None, :] <= local[:, None]) & (local[:, None] < ends[None, :])).astype(
        jnp.int32
    )
    row_start = jnp.sum(inside * starts[None, :], axis=1)
    row_owner = jnp.sum(inside * baseline_owner[None, :], axis=1)
    row_ostart = jnp.sum(inside * owner_start[None, :], axis=1)
    send_slot = row_owner * slot_cap + row_ostart + local - row_start
    outgoing = (
        jnp.zeros((own_slots, feat_width), jnp.bfloat16)
        .at[send_slot]
        .set(tokens)
        .reshape(dp_count, slot_cap, feat_width)
    )
    owner_index = lax.axis_index("dp")
    place = jnp.arange(slot_cap, dtype=jnp.int32)
    held = (
        (baseline_owner[None, :] == owner_index)
        & (owner_start[None, :] <= place[:, None])
        & (place[:, None] < owner_start[None, :] + base_rows[None, :])
    ).astype(jnp.int32)
    got_start = jnp.sum(held * owner_start[None, :], axis=1)
    got_len = jnp.sum(held * base_rows[None, :], axis=1)
    got_id = jnp.sum(held * index[None, :], axis=1)
    got_any = jnp.sum(held, axis=1)
    sender = jnp.arange(dp_count, dtype=jnp.int32)[:, None]
    recv_slot = (
        dp_count * got_start[None, :]
        + sender * got_len[None, :]
        + place[None, :]
        - got_start[None, :]
    )
    recv_slot = jnp.where(got_any[None, :] > 0, recv_slot, own_slots).reshape(-1)
    id_rows = jnp.broadcast_to(got_id[None, :], (dp_count, slot_cap)).reshape(-1)
    slot_ids = jnp.full((own_slots,), -1, jnp.int32).at[recv_slot].set(id_rows, mode="drop")
    arrived = lax.all_to_all(outgoing, "dp", split_axis=0, concat_axis=0, tiled=True)
    width = arrived.shape[-1]
    stream = (
        jnp.zeros((own_slots, width), jnp.bfloat16)
        .at[recv_slot]
        .set(arrived.reshape(-1, width), mode="drop")
    )
    starts_flag = jnp.concatenate(
        [jnp.ones((1,), jnp.int32), (slot_ids[1:] != slot_ids[:-1]).astype(jnp.int32)]
    )
    segment = jnp.cumsum(starts_flag)
    section_idx = lax.axis_index("section")
    params = (
        pre_gain[0],
        input_proj[0],
        gate_proj[0],
        state_proj[0],
        step_proj[0],
        step_bias[0],
        decay_log[0],
        skip_gain[0],
        norm_gain[0],
        out_proj[0],
    )
    local_heads = step_proj.shape[2]
    micro_rows = own_slots // MICRO
    zero_state = (jnp.zeros((local_heads, HEADDIM, NSTATE), jnp.float32), jnp.array(-1, jnp.int32))
    cot_own = cotangent[0]
    carried_state = zero_state
    handed = jnp.zeros((micro_rows, feat_width), jnp.bfloat16)
    outputs_all = jnp.zeros((own_slots, feat_width), jnp.bfloat16)
    grad_acc = jnp.zeros((out_proj.shape[1], feat_width), jnp.float32)
    for turn_index in range(MICRO + 1):
        micro_index = turn_index - section_idx
        active_turn = (micro_index >= 0) & (micro_index < MICRO)
        micro_index = jnp.clip(micro_index, 0, MICRO - 1)
        first_row = micro_index * micro_rows
        own_in = lax.dynamic_slice_in_dim(stream, first_row, micro_rows, 0)
        source = jnp.where(section_idx == 0, own_in, handed)
        seg_part = lax.dynamic_slice_in_dim(segment, first_row, micro_rows, 0)
        result, y_norm, moved = block_layer(source, seg_part, carried_state, params)
        carried_state = jax.tree.map(
            lambda new_val, old_val: jnp.where(active_turn, new_val, old_val), moved, carried_state
        )
        outputs_all = jnp.where(
            active_turn,
            lax.dynamic_update_slice_in_dim(outputs_all, result, first_row, 0),
            outputs_all,
        )
        cot_part = lax.dynamic_slice_in_dim(cot_own, first_row, micro_rows, 0)
        grad_acc = grad_acc + jnp.where(active_turn, grad_term(y_norm, cot_part), 0.0)
        if turn_index < MICRO:
            handed = from_behind(result, "section", 1)
    grad_share = lax.psum_scatter(
        grad_acc.astype(jnp.bfloat16), "dp", scatter_dimension=1, tiled=True
    )
    return (outputs_all[None], grad_share[None])


def solution(mesh):
    return jax.shard_map(
        per_device,
        mesh=mesh,
        in_specs=(
            P("dp", None),
            P(),
            P(),
            P("section", "dp", None),
            P("section", None),
            P("section", None, "tensor"),
            P("section", None, "tensor"),
            P("section", None, None),
            P("section", None, "tensor"),
            P("section", "tensor"),
            P("section", "tensor"),
            P("section", "tensor"),
            P("section", "tensor"),
            P("section", "tensor", None),
        ),
        out_specs=(P("section", "dp", None), P("section", "tensor", "dp")),
        check_vma=False,
    )
```

profile of v0, /device:TPU:2, one launch (start us, length us, event | category | flops | bytes accessed | tf_op | source)
XLA Modules:
  0.0 645.6 jit_solution(3707332609720669846)
XLA Ops:
  7.2 1.0 select_reduce_fusion.3
  10.8 4.4 scatter_custom_fusion
  15.2 11.8 %all-to-all-start = ((bf16[32,16,2048]{2,1,0:T(8,128)(2,1)}), bf16[32,16,2048]{2,1,0:T(8,128)(2,1)}, u32[]{:S(2)}, u32[]{:S(2)}) async-start(bf16[32,16,2048]{2,1,0:T(8,128)(2,1)} %bitcast.297), calls=%async_computation | async-start | bytes 4194304 | tf_op jit(solution)/shard_map/all_to_all | solution.py:203
  28.2 2.4 scatter_custom_fusion.2
  32.2 44.9 %all-to-all-done = bf16[32,16,2048]{2,1,0:T(8,128)(2,1)} async-done(((bf16[32,16,2048]{2,1,0:T(8,128)(2,1)}), bf16[32,16,2048]{2,1,0:T(8,128)(2,1)}, u32[]{:S(2)}, u32[]{:S(2)}) %all-to-all-start) | async-done | bytes 2097184 | tf_op jit(solution)/shard_map/all_to_all | solution.py:203
  77.1 6.1 scatter_custom_fusion.1
  83.2 1.6 multiply_reduce_fusion.2
  84.9 1.7 compare_select_fusion.2
  87.4 2.2 multiply_convert_fusion.20
  91.4 1.1 broadcast.415.clone2
  92.4 33.7 %while.45 = (s32[]{:T(128)}, f32[8,64,128]{2,1,0:T(8,128)S(1)}, s32[]{:T(128)}, f32[4,64,8,64]{3,2,1,0:T(8,128)}, s32[4,64]{1,0:T(4,128)S(1)}, /*index=5*/f32[4,...) while((s32[]{:T(128)}, f32[8,64,128]{2,1,0:T(8,128)S(1)}, ...), condition=%wide.region_17.18_spmd.clone, body=%wide.region_15.17_spmd.clone.sunk | while | flops 22689996 | bytes 2389582 | solution.py:76
  98.6 0.9 convolution_add_fusion.11
  107.0 0.9 convolution_add_fusion.11
  115.4 0.9 convolution_add_fusion.11
  126.2 1.5 reshape.687
  127.7 2.9 multiply_reduce_fusion.5
  130.6 8.6 %psum.21 = f32[256]{0:T(256)S(1)} all-reduce(f32[256]{0:T(256)S(1)} %get-tuple-element.392), channel_id=1, replica_groups=mesh['dp'=32,'section'=2,'tensor'=4] {'tensor'}, use_global_device_ids=true, to_apply=%region_19.20 | all-reduce | flops 256 | bytes 2048 | tf_op jit(solution)/shard_map/psum | solution.py:124
  139.2 3.4 convolution_convert_fusion.2
  142.7 2.8 fusion.116
  145.5 18.4 %reduce-scatter.5.cloned.1.call-done = bf16[64,2048]{1,0:T(8,128)(2,1)} async-done(((bf16[256,2048]{1,0:T(8,128)(2,1)}), bf16[64,2048]{1,0:T(8,128)(2,1)}) %reduce-scatter.5.cloned.1.call-update) | async-done | bytes 262160 | tf_op jit(solution)/shard_map/reduce_scatter | solution.py:129
  163.9 1.9 add_convert_fusion.3
  165.9 27.4 %all-gather.4.cloned.1.call-done = bf16[256,2048]{1,0:T(8,128)(2,1)} async-done(((bf16[64,2048]{1,0:T(8,128)(2,1)}), bf16[256,2048]{1,0:T(8,128)(2,1)}) %all-gather.4.cloned.1.call-update) | async-done | bytes 1048592 | tf_op jit(solution)/shard_map/all_gather | solution.py:137
  193.3 2.3 collective-permute-start
  196.3 0.9 collective-permute-done
  197.2 3.0 fusion.154
  202.4 1.0 copy-done.28
  204.4 1.1 reshape_reshape.10
  205.5 1.0 broadcast.415.clone2.1
  206.5 30.9 %while.43 = (s32[]{:T(128)}, f32[8,64,128]{2,1,0:T(8,128)S(1)}, s32[]{:T(128)}, f32[4,64,8,64]{3,2,1,0:T(8,128)}, s32[4,64]{1,0:T(4,128)}, /*index=5*/f32[4,64,8...) while((s32[]{:T(128)}, f32[8,64,128]{2,1,0:T(8,128)S(1)}, ...), condition=%wide.region_24.25_spmd, body=%wide.region_22.24_spmd.sunk | while | flops 22624460 | bytes 2581539 | solution.py:76
  210.3 0.9 constant_dynamic-slice_fusion.12
  218.0 0.9 constant_dynamic-slice_fusion.12
  225.8 0.9 constant_dynamic-slice_fusion.12
  233.5 0.9 constant_dynamic-slice_fusion.12
  237.4 2.3 reshape.692
  239.7 3.0 multiply_reduce_fusion.4
  242.8 9.2 %psum.22 = f32[256]{0:T(256)S(1)} all-reduce(f32[256]{0:T(256)S(1)} %get-tuple-element.394), channel_id=1, replica_groups=mesh['dp'=32,'section'=2,'tensor'=4] {'tensor'}, use_global_device_ids=true, to_apply=%region_26.27 | all-reduce | flops 256 | bytes 2048 | tf_op jit(solution)/shard_map/psum | solution.py:124
  252.0 3.3 convolution_convert_fusion.1
  255.4 24.6 %reduce-scatter.7.cloned.1.call-done = bf16[64,2048]{1,0:T(8,128)(2,1)} async-done(((bf16[256,2048]{1,0:T(8,128)(2,1)}), bf16[64,2048]{1,0:T(8,128)(2,1)}) %reduce-scatter.7.cloned.1.call-update) | async-done | bytes 262160 | tf_op jit(solution)/shard_map/reduce_scatter | solution.py:129
  280.0 1.9 add_convert_fusion.2
  282.0 27.4 %all-gather.6.cloned.1.call-done = bf16[256,2048]{1,0:T(8,128)(2,1)} async-done(((bf16[64,2048]{1,0:T(8,128)(2,1)}), bf16[256,2048]{1,0:T(8,128)(2,1)}) %all-gather.6.cloned.1.call-update) | async-done | bytes 1048592 | tf_op jit(solution)/shard_map/all_gather | solution.py:137
  309.4 2.3 collective-permute-start.1
  311.8 1.5 collective-permute-done.1
  313.3 3.0 fusion.153
  318.5 1.0 copy-done.29
  320.5 1.1 reshape_reshape.11
  321.6 1.0 broadcast.415.clone
  322.6 22.8 %while.44 = (s32[]{:T(128)}, f32[8,64,128]{2,1,0:T(8,128)S(1)}, s32[]{:T(128)}, f32[4,64,8,64]{3,2,1,0:T(8,128)}, s32[4,64]{1,0:T(4,128)S(1)}, /*index=5*/f32[4,...) while((s32[]{:T(128)}, f32[8,64,128]{2,1,0:T(8,128)S(1)}, ...), condition=%wide.region_31.32_spmd, body=%wide.region_29.31_spmd.sunk | while | flops 22624460 | bytes 2582019 | solution.py:76
  325.1 0.9 constant_dynamic-slice_fusion.13
  330.7 0.9 constant_dynamic-slice_fusion.13
  336.4 0.9 constant_dynamic-slice_fusion.13
  342.1 0.9 constant_dynamic-slice_fusion.13
  345.4 1.5 reshape.697
  346.9 2.8 multiply_reduce_fusion.3
  349.8 9.2 %psum.23 = f32[256]{0:T(256)S(1)} all-reduce(f32[256]{0:T(256)S(1)} %get-tuple-element.396), channel_id=1, replica_groups=mesh['dp'=32,'section'=2,'tensor'=4] {'tensor'}, use_global_device_ids=true, to_apply=%region_33.34 | all-reduce | flops 256 | bytes 2048 | tf_op jit(solution)/shard_map/psum | solution.py:124
  359.0 3.3 convolution_convert_fusion
  362.4 24.6 %reduce-scatter.9.cloned.1.call-done = bf16[64,2048]{1,0:T(8,128)(2,1)} async-done(((bf16[256,2048]{1,0:T(8,128)(2,1)}), bf16[64,2048]{1,0:T(8,128)(2,1)}) %reduce-scatter.9.cloned.1.call-update) | async-done | bytes 262160 | tf_op jit(solution)/shard_map/reduce_scatter | solution.py:129
  387.0 1.9 add_convert_fusion.1
  390.9 2.5 add_convert_fusion
  393.6 0.9 copy-done.10
  395.3 1.3 copy-done.1
  396.6 1.3 copy.198
  397.9 18.4 %all-gather.8.cloned.1.call-done = bf16[256,2048]{1,0:T(8,128)(2,1)} async-done(((bf16[64,2048]{1,0:T(8,128)(2,1)}), bf16[256,2048]{1,0:T(8,128)(2,1)}) %all-gather.8.cloned.1.call-update) | async-done | bytes 1048592 | tf_op jit(solution)/shard_map/all_gather | solution.py:137
  416.4 2.6 bitcast_dynamic-update-slice_fusion
  419.0 219.8 %reduce-scatter.11.cloned.1.call-done = bf16[512,64]{0,1:T(8,128)(2,1)} async-done(((bf16[512,2048]{0,1:T(8,128)(2,1)}), bf16[512,64]{0,1:T(8,128)(2,1)}) %reduce-scatter.11.cloned.1.call-update) | async-done | bytes 65552 | tf_op jit(solution)/shard_map/reduce_scatter | solution.py:256
  (407 shorter events, 79.5 us)
Async XLA Ops:
  7.2 381.8 %copy-start = (bf16[1,512,2048]{2,1,0:T(8,128)(2,1)S(1)}, bf16[1,512,2048]{2,1,0:T(8,128)(2,1)}, u32[]{:S(2)}) copy-start(bf16[1,512,2048]{2,1,0:T(8,128)(2,1)} %param.23) | copy-start | bytes 6291460
  15.2 11.9 %copy-start.26 = (f32[1,8]{1,0:T(1,128)S(1)}, f32[1,8]{1,0:T(1,128)}, u32[]{:S(2)}) copy-start(f32[1,8]{1,0:T(1,128)} %param.31) | copy-start | bytes 100
  15.2 12.6 %copy-start.20 = (s32[128]{0:T(128)S(1)}, s32[128]{0:T(128)}, u32[]{:S(2)}) copy-start(s32[128]{0:T(128)} %param.22) | copy-start | bytes 1540
  15.2 12.7 %copy-start.19 = (s32[128]{0:T(128)S(1)}, s32[128]{0:T(128)}, u32[]{:S(2)}) copy-start(s32[128]{0:T(128)} %param.21) | copy-start | bytes 1540
  15.2 17.0 %copy-start.38 = (f32[1,8]{1,0:T(1,128)S(1)}, f32[1,8]{1,0:T(1,128)}, u32[]{:S(2)}) copy-start(f32[1,8]{1,0:T(1,128)} %param.30) | copy-start | bytes 100
  15.2 61.9 %all-to-all-start = ((bf16[32,16,2048]{2,1,0:T(8,128)(2,1)}), bf16[32,16,2048]{2,1,0:T(8,128)(2,1)}, u32[]{:S(2)}, u32[]{:S(2)}) async-start(bf16[32,16,2048]{2,1,0:T(8,128)(2,1)} %bitcast.297), calls=%async_computation | async-start | bytes 4194304 | tf_op jit(solution)/shard_map/all_to_all | solution.py:203
  27.0 57.9 %copy-start.32 = (bf16[1,2048,8]{1,2,0:T(8,128)(2,1)S(1)}, bf16[1,2048,8]{1,2,0:T(8,128)(2,1)}, u32[]{:S(2)}) copy-start(bf16[1,2048,8]{1,2,0:T(8,128)(2,1)} %param.28) | copy-start | bytes 98308
  27.0 57.9 %copy-start.35 = (f32[1,2048]{1,0:T(1,128)S(1)}, f32[1,2048]{1,0:T(1,128)}, u32[]{:S(2)}) copy-start(f32[1,2048]{1,0:T(1,128)} %param.24) | copy-start | bytes 24580
  27.0 57.9 %copy-start.39 = (f32[1,8]{1,0:T(1,128)S(1)}, f32[1,8]{1,0:T(1,128)}, u32[]{:S(2)}) copy-start(f32[1,8]{1,0:T(1,128)} %param.29) | copy-start | bytes 100
  27.0 137.0 %reduce-scatter.5.cloned.1.call-start = ((), (), s32[]{:S(2)}) async-start(), calls=%async_computation.5 | async-start | bytes 1310720 | tf_op jit(solution)/shard_map/reduce_scatter | solution.py:129
  84.8 5.4 copy-start.24
  87.4 2.9 copy-start.2
  87.4 2.9 copy-start.27
  91.1 1.4 copy-start.14
  92.4 4.2 copy-start.17
  97.5 2.7 copy-start.18
  100.8 4.3 copy-start.17
  105.9 2.7 copy-start.18
  109.3 4.3 copy-start.17
  114.4 2.7 copy-start.18
  117.7 4.3 copy-start.17
  122.8 2.7 copy-start.18
  127.7 11.6 %copy-start.11 = (f32[1,512]{1,0:T(1,128)S(1)}, f32[1,512]{1,0:T(1,128)}, u32[]{:S(2)}) copy-start(f32[1,512]{1,0:T(1,128)} %param.32) | copy-start | bytes 6148
  130.5 12.0 %copy-start.5 = (f32[256,512]{1,0:T(8,128)}, f32[256,512]{1,0:T(8,128)S(1)}, u32[]{:S(2)}) copy-start(f32[256,512]{1,0:T(8,128)S(1)} %get-tuple-element.393) | copy-start | bytes 1572868
  139.2 3.4 copy-start.15
  142.6 50.7 %all-gather.4.cloned.1.call-start = ((), (), s32[]{:S(2)}) async-start(), calls=%async_computation.6 | async-start | bytes 1310720 | tf_op jit(solution)/shard_map/all_gather | solution.py:137
  142.7 52.9 %copy-start.22 = (s32[256]{0:T(256)S(1)}, s32[256]{0:T(256)}, u32[]{:S(2)}) copy-start(s32[256]{0:T(256)} %get-tuple-element.388) | copy-start | bytes 3076
  165.9 114.2 %reduce-scatter.7.cloned.1.call-start = ((), (), s32[]{:S(2)}) async-start(), calls=%async_computation.7 | async-start | bytes 1310720 | tf_op jit(solution)/shard_map/reduce_scatter | solution.py:129
  193.3 3.9 collective-permute-start
  196.3 4.3 copy-start.33
  196.3 4.3 copy-start.36
  196.3 4.3 copy-start.40
  200.2 2.2 copy-start.4
  200.2 1.6 copy-start.30
  200.5 1.8 copy-start.25
  201.8 1.6 copy-start.28
  204.2 2.3 copy-start.13
  242.8 12.6 %copy-start.7 = (f32[256,512]{1,0:T(8,128)}, f32[256,512]{1,0:T(8,128)S(1)}, u32[]{:S(2)}) copy-start(f32[256,512]{1,0:T(8,128)S(1)} %get-tuple-element.395) | copy-start | bytes 1572868
  255.3 56.3 %copy-start.21 = (s32[256]{0:T(256)S(1)}, s32[256]{0:T(256)}, u32[]{:S(2)}) copy-start(s32[256]{0:T(256)} %get-tuple-element.387) | copy-start | bytes 3076
  255.4 54.0 %all-gather.6.cloned.1.call-start = ((), (), s32[]{:S(2)}) async-start(), calls=%async_computation.8 | async-start | bytes 1310720 | tf_op jit(solution)/shard_map/all_gather | solution.py:137
  281.9 105.1 %reduce-scatter.9.cloned.1.call-start = ((), (), s32[]{:S(2)}) async-start(), calls=%async_computation.9 | async-start | bytes 1310720 | tf_op jit(solution)/shard_map/reduce_scatter | solution.py:129
  309.4 3.9 collective-permute-start.1
  311.8 4.8 copy-start.34
  311.8 4.8 copy-start.37
  311.8 4.8 copy-start.41
  316.3 2.2 copy-start.3
  316.3 1.6 copy-start.31
  317.9 1.6 copy-start.29
  320.3 2.3 copy-start.12
  322.6 24.3 %copy-start.23 = (f32[512]{0:T(512)S(1)}, f32[512]{0:T(512)}, u32[]{:S(2)}) copy-start(f32[512]{0:T(512)} %mul.547) | copy-start | bytes 6148
  362.3 26.7 %copy-start.6 = (f32[256,512]{1,0:T(8,128)S(1)}, f32[256,512]{1,0:T(8,128)}, u32[]{:S(2)}) copy-start(f32[256,512]{1,0:T(8,128)} %copy-done.5) | copy-start | bytes 1572868
  362.3 26.7 %copy-start.16 = (f32[256]{0:T(256)S(1)}, f32[256]{0:T(256)}, u32[]{:S(2)}) copy-start(f32[256]{0:T(256)} %copy-done.15) | copy-start | bytes 3076
  362.3 54.0 %all-gather.8.cloned.1.call-start = ((), (), s32[]{:S(2)}) async-start(), calls=%async_computation.10 | async-start | bytes 1310720 | tf_op jit(solution)/shard_map/all_gather | solution.py:137
  388.9 249.8 %reduce-scatter.11.cloned.1.call-start = ((), (), s32[]{:S(2)}) async-start(), calls=%async_computation.11 | async-start | bytes 2162688 | tf_op jit(solution)/shard_map/reduce_scatter | solution.py:256
  389.0 1.0 copy-start.8
  393.3 1.2 copy-start.10
  393.4 1.5 copy-start.9
  395.3 1.3 copy-start.1
Sparse Core Ops, SparseCore 0:
  142.7 21.1 reduce-scatter.4
  166.0 27.2 all-gather.3
  255.5 24.5 reduce-scatter.6
  282.0 27.2 all-gather.5
  362.5 24.5 reduce-scatter.8
  389.1 27.2 all-gather.7
  421.2 217.4 reduce-scatter.10
where the time goes:
time: 648 us; the launch traced here: 646 us
  waiting for transfers between devices  408 us (63%)
  local copies, waits for them, and re-layouts  66.8 us (10%)
  matrix products  51.8 us (8%)
  other arithmetic  44.7 us (7%)
  blocking collectives  27 us (4%)
  starting transfers between devices  16.6 us (3%)
  loops' own time  15.7 us (2%)
  between operations  14.8 us (2%)
    reduce_scatter x1, waiting for transfers between devices, per_device(): lax.psum_scatter(grad_acc.astype(jnp.bfloat16), 'dp', scatter_dimension=1...  220 us
    all_gather x3, waiting for transfers between devices, block_layer(): result = lax.all_gather(own_out, 'tensor', axis=0, tiled=True)  73.3 us
    reduce_scatter x3, waiting for transfers between devices, block_layer(): lax.psum_scatter(jnp.dot(y_norm, out_proj, preferred_element_type=jnp.flo...  67.7 us
    all_to_all x1, waiting for transfers between devices, per_device(): lax.all_to_all(outgoing, 'dp', split_axis=0, concat_axis=0, tiled=True)  44.9 us
    psum x3, blocking collectives, block_layer(): sq_sum = lax.psum(jnp.sum(gated * gated, axis=-1), 'tensor')  27 us
    another operation x3, loops' own time, block_scan(): lax.scan(advance, (state, prev_segment), scanned)  15.7 us
  transfers between devices with their start and end apart: 10, of which 10 were waited for; matrix products, arithmetic and copies ran while one was open for 3% of the time, Pallas kernels for 0%

commit v1 on v0

--- a/solution.py
+++ b/solution.py
@@ -134,7 +134,9 @@
     ).astype(jnp.float32)
     own_rows = lax.dynamic_slice_in_dim(rows_f, lax.axis_index("tensor") * row_share, row_share, 0)
     own_out = (own_rows + summed).astype(jnp.bfloat16)
-    result = lax.all_gather(own_out, "tensor", axis=0, tiled=True)
+    result = jnp.concatenate(
+        lax.all_to_all(jnp.stack([own_out] * lax.axis_size("tensor")), "tensor", 0, 0), axis=0
+    )
     return (result, y_norm, (state_end, segment_end))
 
 

time: 648 us -> 600 us (0.926)
  waiting for transfers between devices: 408 us -> 316 us
  blocking collectives: 27 us -> 63.3 us
    all_gather x3 -> x0, waiting for transfers between devices: 73.3 us -> none  [block_layer(): result = lax.all_gather(own_out, 'tensor', axis=0, tiled=True)]
    all_to_all x0 -> x2, blocking collectives: none -> 36.3 us  [block_layer(): lax.all_to_all(jnp.stack([own_out] * lax.axis_size('tensor')), 'tensor',...]
    reduce_scatter x1, waiting for transfers between devices: 220 us -> 199 us  [per_device(): lax.psum_scatter(grad_acc.astype(jnp.bfloat16), 'dp', scatter_dimension=1...]
    all_to_all x0 -> x1, waiting for transfers between devices: none -> 6.62 us  [block_layer(): lax.all_to_all(jnp.stack([own_out] * lax.axis_size('tensor')), 'tensor',...]
  transfers between devices with their start and end apart: 10 -> 8, of which waited for: 10 -> 8; matrix products, arithmetic and copies ran while one was open for 3% -> 4% of each run, Pallas kernels for 0% -> 0%
where the time goes in v1:
time: 600 us; the launch traced here: 597 us
  waiting for transfers between devices  316 us (53%)
  local copies, waits for them, and re-layouts  67.7 us (11%)
  blocking collectives  63.3 us (11%)
  matrix products  51.8 us (9%)
  other arithmetic  45.3 us (8%)
  starting transfers between devices  22.4 us (4%)
  loops' own time  16.7 us (3%)
  between operations  14.5 us (2%)
    reduce_scatter x1, waiting for transfers between devices, per_device(): lax.psum_scatter(grad_acc.astype(jnp.bfloat16), 'dp', scatter_dimension=1...  199 us
    reduce_scatter x3, waiting for transfers between devices, block_layer(): lax.psum_scatter(jnp.dot(y_norm, out_proj, preferred_element_type=jnp.flo...  62.5 us
    all_to_all x1, waiting for transfers between devices, per_device(): lax.all_to_all(outgoing, 'dp', split_axis=0, concat_axis=0, tiled=True)  44.9 us
    all_to_all x2, blocking collectives, block_layer(): lax.all_to_all(jnp.stack([own_out] * lax.axis_size('tensor')), 'tensor',...  36.3 us
    psum x3, blocking collectives, block_layer(): sq_sum = lax.psum(jnp.sum(gated * gated, axis=-1), 'tensor')  27 us
    another operation x3, loops' own time, block_scan(): lax.scan(advance, (state, prev_segment), scanned)  16.7 us
  transfers between devices with their start and end apart: 8, of which 8 were waited for; matrix products, arithmetic and copies ran while one was open for 4% of the time, Pallas kernels for 0%

profile of v1, /device:TPU:2, one launch (start us, length us, event | category | flops | bytes accessed | tf_op | source)
XLA Modules:
  0.0 597.4 jit_solution(10268470663560738328)
XLA Ops:
  7.2 1.0 select_reduce_fusion.3
  10.8 4.4 scatter_custom_fusion
  15.2 11.8 %all-to-all-start = ((bf16[32,16,2048]{2,1,0:T(8,128)(2,1)}), bf16[32,16,2048]{2,1,0:T(8,128)(2,1)}, u32[]{:S(2)}, u32[]{:S(2)}) async-start(bf16[32,16,2048]{2,1,0:T(8,128)(2,1)} %bitcast.301), calls=%async_computation | async-start | bytes 4194304 | tf_op jit(solution)/shard_map/all_to_all | solution.py:205
  28.2 2.4 scatter_custom_fusion.2
  32.2 44.9 %all-to-all-done = bf16[32,16,2048]{2,1,0:T(8,128)(2,1)} async-done(((bf16[32,16,2048]{2,1,0:T(8,128)(2,1)}), bf16[32,16,2048]{2,1,0:T(8,128)(2,1)}, u32[]{:S(2)}, u32[]{:S(2)}) %all-to-all-start) | async-done | bytes 2097184 | tf_op jit(solution)/shard_map/all_to_all | solution.py:205
  77.1 6.1 %scatter_custom_fusion.1 = bf16[512,2048]{1,0:T(8,128)(2,1)} fusion(s32[512]{0:T(512)S(1)} %bitcast.321, bf16[512,2048]{1,0:T(8,128)(2,1)} %bitcast.30, bf16[]{:T(256)} %constant.123.clone.1), kind=kCustom, calls=%fused_computation.184 | custom fusion | bytes 2097664 | tf_op jit(solution)/shard_map/scatter | solution.py:210
  83.2 1.6 multiply_reduce_fusion.2
  84.9 1.7 compare_select_fusion.2
  87.4 2.2 multiply_convert_fusion.20
  91.4 1.1 broadcast.421.clone2
  92.4 32.7 %while.45 = (s32[]{:T(128)}, f32[8,64,128]{2,1,0:T(8,128)S(1)}, s32[]{:T(128)}, f32[4,64,8,64]{3,2,1,0:T(8,128)}, s32[4,64]{1,0:T(4,128)S(1)}, /*index=5*/f32[4,...) while((s32[]{:T(128)}, f32[8,64,128]{2,1,0:T(8,128)S(1)}, ...), condition=%wide.region_17.18_spmd.clone, body=%wide.region_15.17_spmd.clone.sunk | while | flops 22689996 | bytes 2389582 | solution.py:76
  125.2 1.5 reshape.702
  126.7 2.9 multiply_reduce_fusion.5
  129.6 8.6 %psum.21 = f32[256]{0:T(256)S(1)} all-reduce(f32[256]{0:T(256)S(1)} %get-tuple-element.392), channel_id=1, replica_groups=mesh['dp'=32,'section'=2,'tensor'=4] {'tensor'}, use_global_device_ids=true, to_apply=%region_19.20 | all-reduce | flops 256 | bytes 2048 | tf_op jit(solution)/shard_map/psum | solution.py:124
  138.2 3.4 convolution_convert_fusion.2
  141.6 2.8 fusion.116
  144.5 18.5 %reduce-scatter.5.cloned.1.call-done = bf16[64,2048]{1,0:T(8,128)(2,1)} async-done(((bf16[256,2048]{1,0:T(8,128)(2,1)}), bf16[64,2048]{1,0:T(8,128)(2,1)}) %reduce-scatter.5.cloned.1.call-update) | async-done | bytes 262160 | tf_op jit(solution)/shard_map/reduce_scatter | solution.py:129
  163.0 1.2 add_convert_fusion.3
  164.3 18.1 %all_to_all.20 = bf16[4,64,2048]{2,1,0:T(8,128)(2,1)} all-to-all(bf16[4,64,2048]{2,1,0:T(8,128)(2,1)S(1)} %stack.6), channel_id=1, replica_groups=mesh['dp'=32,'section'=2,'tensor'=4] {'tensor'}, dimensions={0} | all-to-all | bytes 2097152 | tf_op jit(solution)/shard_map/all_to_all | solution.py:138
  182.4 2.3 collective-permute-start
  185.4 0.9 collective-permute-done
  186.3 3.0 fusion.154
  191.5 1.0 copy-done.32
  193.5 1.1 reshape_reshape.10
  194.6 1.0 broadcast.421.clone2.1
  195.6 31.7 %while.43 = (s32[]{:T(128)}, f32[8,64,128]{2,1,0:T(8,128)S(1)}, s32[]{:T(128)}, f32[4,64,8,64]{3,2,1,0:T(8,128)}, s32[4,64]{1,0:T(4,128)}, /*index=5*/f32[4,64,8...) while((s32[]{:T(128)}, f32[8,64,128]{2,1,0:T(8,128)S(1)}, ...), condition=%wide.region_24.25_spmd, body=%wide.region_22.24_spmd.sunk | while | flops 22624460 | bytes 2581539 | solution.py:76
  199.6 0.9 constant_dynamic-slice_fusion.12
  207.5 0.9 constant_dynamic-slice_fusion.12
  215.4 0.9 constant_dynamic-slice_fusion.12
  223.4 0.9 constant_dynamic-slice_fusion.12
  227.3 2.3 reshape.708
  229.6 3.0 multiply_reduce_fusion.4
  232.7 9.2 %psum.22 = f32[256]{0:T(256)S(1)} all-reduce(f32[256]{0:T(256)S(1)} %get-tuple-element.394), channel_id=1, replica_groups=mesh['dp'=32,'section'=2,'tensor'=4] {'tensor'}, use_global_device_ids=true, to_apply=%region_26.27 | all-reduce | flops 256 | bytes 2048 | tf_op jit(solution)/shard_map/psum | solution.py:124
  241.9 3.4 convolution_convert_fusion.1
  245.4 24.2 %reduce-scatter.7.cloned.1.call-done = bf16[64,2048]{1,0:T(8,128)(2,1)} async-done(((bf16[256,2048]{1,0:T(8,128)(2,1)}), bf16[64,2048]{1,0:T(8,128)(2,1)}) %reduce-scatter.7.cloned.1.call-update) | async-done | bytes 262160 | tf_op jit(solution)/shard_map/reduce_scatter | solution.py:129
  269.6 1.2 add_convert_fusion.2
  270.9 18.2 %all_to_all.21 = bf16[4,64,2048]{2,1,0:T(8,128)(2,1)} all-to-all(bf16[4,64,2048]{2,1,0:T(8,128)(2,1)S(1)} %stack.7), channel_id=1, replica_groups=mesh['dp'=32,'section'=2,'tensor'=4] {'tensor'}, dimensions={0} | all-to-all | bytes 2097152 | tf_op jit(solution)/shard_map/all_to_all | solution.py:138
  289.1 2.3 collective-permute-start.1
  291.5 1.5 collective-permute-done.1
  293.0 3.0 fusion.153
  298.1 1.0 copy-done.33
  300.2 1.1 reshape_reshape.11
  301.2 1.1 broadcast.421.clone
  302.3 24.7 %while.44 = (s32[]{:T(128)}, f32[8,64,128]{2,1,0:T(8,128)S(1)}, s32[]{:T(128)}, f32[4,64,8,64]{3,2,1,0:T(8,128)}, s32[4,64]{1,0:T(4,128)S(1)}, /*index=5*/f32[4,...) while((s32[]{:T(128)}, f32[8,64,128]{2,1,0:T(8,128)S(1)}, ...), condition=%wide.region_31.32_spmd, body=%wide.region_29.31_spmd.sunk | while | flops 22624460 | bytes 2590267 | solution.py:76
  305.1 0.9 constant_dynamic-slice_fusion.13
  311.3 0.9 constant_dynamic-slice_fusion.13
  317.5 0.9 constant_dynamic-slice_fusion.13
  323.6 0.9 constant_dynamic-slice_fusion.13
  327.0 1.5 reshape.714
  328.5 2.9 multiply_reduce_fusion.3
  331.4 9.2 %psum.23 = f32[256]{0:T(256)S(1)} all-reduce(f32[256]{0:T(256)S(1)} %get-tuple-element.396), channel_id=1, replica_groups=mesh['dp'=32,'section'=2,'tensor'=4] {'tensor'}, use_global_device_ids=true, to_apply=%region_33.34 | all-reduce | flops 256 | bytes 2048 | tf_op jit(solution)/shard_map/psum | solution.py:124
  340.6 3.4 convolution_convert_fusion
  346.0 2.4 add_convert_fusion
  348.4 19.7 %reduce-scatter.9.cloned.1.call-done = bf16[64,2048]{1,0:T(8,128)(2,1)} async-done(((bf16[256,2048]{1,0:T(8,128)(2,1)}), bf16[64,2048]{1,0:T(8,128)(2,1)}) %reduce-scatter.9.cloned.1.call-update) | async-done | bytes 262160 | tf_op jit(solution)/shard_map/reduce_scatter | solution.py:129
  368.1 1.2 add_convert_fusion.1
  369.3 1.1 stack.8
  370.4 5.9 all-to-all-start.3
  376.6 1.5 select_dynamic-update-slice_fusion.1
  378.0 1.6 select_dynamic-update-slice_fusion
  379.7 1.3 copy-done.1
  381.0 1.3 copy.198
  382.3 6.6 %all-to-all-done.3 = bf16[4,64,2048]{2,1,0:T(8,128)(2,1)S(1)} async-done(((bf16[4,64,2048]{2,1,0:T(8,128)(2,1)}), bf16[4,64,2048]{2,1,0:T(8,128)(2,1)S(1)}, u32[]{:S(2)}, u32[]{:S(2)}) %all-to-all-start.3) | async-done | bytes 1048608 | tf_op jit(solution)/shard_map/all_to_all | solution.py:138
  389.0 2.6 bitcast_dynamic-update-slice_fusion
  391.5 199.3 %reduce-scatter.11.cloned.1.call-done = bf16[512,64]{0,1:T(8,128)(2,1)} async-done(((bf16[512,2048]{0,1:T(8,128)(2,1)}), bf16[512,64]{0,1:T(8,128)(2,1)}) %reduce-scatter.11.cloned.1.call-update) | async-done | bytes 65552 | tf_op jit(solution)/shard_map/reduce_scatter | solution.py:258
  (427 shorter events, 82.3 us)
Async XLA Ops:
  7.2 336.9 %copy-start = (bf16[1,512,2048]{2,1,0:T(8,128)(2,1)S(1)}, bf16[1,512,2048]{2,1,0:T(8,128)(2,1)}, u32[]{:S(2)}) copy-start(bf16[1,512,2048]{2,1,0:T(8,128)(2,1)} %param.23) | copy-start | bytes 6291460
  15.2 11.9 %copy-start.30 = (f32[1,8]{1,0:T(1,128)S(1)}, f32[1,8]{1,0:T(1,128)}, u32[]{:S(2)}) copy-start(f32[1,8]{1,0:T(1,128)} %param.31) | copy-start | bytes 100
  15.2 12.6 %copy-start.22 = (s32[128]{0:T(128)S(1)}, s32[128]{0:T(128)}, u32[]{:S(2)}) copy-start(s32[128]{0:T(128)} %param.22) | copy-start | bytes 1540
  15.2 12.7 %copy-start.21 = (s32[128]{0:T(128)S(1)}, s32[128]{0:T(128)}, u32[]{:S(2)}) copy-start(s32[128]{0:T(128)} %param.21) | copy-start | bytes 1540
  15.2 17.0 %copy-start.43 = (f32[1,8]{1,0:T(1,128)S(1)}, f32[1,8]{1,0:T(1,128)}, u32[]{:S(2)}) copy-start(f32[1,8]{1,0:T(1,128)} %param.30) | copy-start | bytes 100
  15.2 61.9 %all-to-all-start = ((bf16[32,16,2048]{2,1,0:T(8,128)(2,1)}), bf16[32,16,2048]{2,1,0:T(8,128)(2,1)}, u32[]{:S(2)}, u32[]{:S(2)}) async-start(bf16[32,16,2048]{2,1,0:T(8,128)(2,1)} %bitcast.301), calls=%async_computation | async-start | bytes 4194304 | tf_op jit(solution)/shard_map/all_to_all | solution.py:205
  27.0 57.9 %copy-start.36 = (bf16[1,2048,8]{1,2,0:T(8,128)(2,1)S(1)}, bf16[1,2048,8]{1,2,0:T(8,128)(2,1)}, u32[]{:S(2)}) copy-start(bf16[1,2048,8]{1,2,0:T(8,128)(2,1)} %param.28) | copy-start | bytes 98308
  27.0 57.9 %copy-start.39 = (f32[1,2048]{1,0:T(1,128)S(1)}, f32[1,2048]{1,0:T(1,128)}, u32[]{:S(2)}) copy-start(f32[1,2048]{1,0:T(1,128)} %param.24) | copy-start | bytes 24580
  27.0 57.9 %copy-start.44 = (f32[1,8]{1,0:T(1,128)S(1)}, f32[1,8]{1,0:T(1,128)}, u32[]{:S(2)}) copy-start(f32[1,8]{1,0:T(1,128)} %param.29) | copy-start | bytes 100
  27.0 136.0 %reduce-scatter.5.cloned.1.call-start = ((), (), s32[]{:S(2)}) async-start(), calls=%async_computation.8 | async-start | bytes 1310720 | tf_op jit(solution)/shard_map/reduce_scatter | solution.py:129
  84.8 5.4 copy-start.28
  87.4 2.9 copy-start.2
  87.4 2.9 copy-start.31
  91.1 1.4 copy-start.12
  92.4 4.1 copy-start.19
  97.3 2.7 copy-start.20
  100.6 4.1 copy-start.19
  105.5 2.7 copy-start.20
  108.8 4.1 copy-start.19
  113.7 2.7 copy-start.20
  117.0 4.1 copy-start.19
  121.9 2.7 copy-start.20
  126.7 11.5 %copy-start.9 = (f32[1,512]{1,0:T(1,128)S(1)}, f32[1,512]{1,0:T(1,128)}, u32[]{:S(2)}) copy-start(f32[1,512]{1,0:T(1,128)} %param.32) | copy-start | bytes 6148
  129.5 12.0 %copy-start.5 = (f32[256,512]{1,0:T(8,128)}, f32[256,512]{1,0:T(8,128)S(1)}, u32[]{:S(2)}) copy-start(f32[256,512]{1,0:T(8,128)S(1)} %get-tuple-element.393) | copy-start | bytes 1572868
  138.2 3.4 copy-start.13
  141.6 128.0 %reduce-scatter.7.cloned.1.call-start = ((), (), s32[]{:S(2)}) async-start(), calls=%async_computation.9 | async-start | bytes 1310720 | tf_op jit(solution)/shard_map/reduce_scatter | solution.py:129
  144.5 40.2 %copy-start.24 = (s32[256]{0:T(256)S(1)}, s32[256]{0:T(256)}, u32[]{:S(2)}) copy-start(s32[256]{0:T(256)} %get-tuple-element.388) | copy-start | bytes 3076
  182.4 3.9 collective-permute-start
  185.3 4.3 copy-start.37
  185.3 4.3 copy-start.40
  185.4 4.2 copy-start.45
  189.3 2.2 copy-start.4
  189.3 1.6 copy-start.34
  189.6 1.8 copy-start.29
  190.9 1.6 copy-start.32
  193.3 2.3 copy-start.11
  232.7 12.6 %copy-start.7 = (f32[256,512]{1,0:T(8,128)}, f32[256,512]{1,0:T(8,128)S(1)}, u32[]{:S(2)}) copy-start(f32[256,512]{1,0:T(8,128)S(1)} %get-tuple-element.395) | copy-start | bytes 1572868
  241.9 3.4 copy-start.15
  245.3 122.8 %reduce-scatter.9.cloned.1.call-start = ((), (), s32[]{:S(2)}) async-start(), calls=%async_computation.10 | async-start | bytes 1310720 | tf_op jit(solution)/shard_map/reduce_scatter | solution.py:129
  269.6 21.8 %copy-start.23 = (s32[256]{0:T(256)S(1)}, s32[256]{0:T(256)}, u32[]{:S(2)}) copy-start(s32[256]{0:T(256)} %get-tuple-element.387) | copy-start | bytes 3076
  289.1 3.9 collective-permute-start.1
  291.4 4.8 copy-start.38
  291.5 4.8 copy-start.41
  291.5 4.8 copy-start.46
  296.0 2.2 copy-start.3
  296.0 1.6 copy-start.35
  296.3 1.8 copy-start.26
  297.6 1.6 copy-start.33
  300.0 2.3 copy-start.10
  302.3 26.2 %copy-start.25 = (f32[512]{0:T(512)S(1)}, f32[512]{0:T(512)}, u32[]{:S(2)}) copy-start(f32[512]{0:T(512)} %mul.547) | copy-start | bytes 6148
  302.3 26.2 %copy-start.27 = (f32[256]{0:T(256)S(1)}, f32[256]{0:T(256)}, u32[]{:S(2)}) copy-start(f32[256]{0:T(256)} %copy-done.26) | copy-start | bytes 3076
  302.3 26.2 %copy-start.42 = (f32[1,2048]{1,0:T(1,128)S(1)}, f32[1,2048]{1,0:T(1,128)}, u32[]{:S(2)}) copy-start(f32[1,2048]{1,0:T(1,128)} %param.24) | copy-start | bytes 24580
  302.3 2.4 copy-start.17
  306.5 1.3 copy-start.18
  308.5 2.4 copy-start.17
  312.7 1.3 copy-start.18
  314.7 2.4 copy-start.17
  320.8 2.4 copy-start.17
  325.0 1.3 copy-start.18
  340.6 3.5 copy-start.6
  340.6 3.5 copy-start.14
  344.0 246.8 %reduce-scatter.11.cloned.1.call-start = ((), (), s32[]{:S(2)}) async-start(), calls=%async_computation.11 | async-start | bytes 2162688 | tf_op jit(solution)/shard_map/reduce_scatter | solution.py:258
  370.4 18.5 %all-to-all-start.3 = ((bf16[4,64,2048]{2,1,0:T(8,128)(2,1)}), bf16[4,64,2048]{2,1,0:T(8,128)(2,1)S(1)}, u32[]{:S(2)}, u32[]{:S(2)}) async-start(bf16[4,64,2048]{2,1,0:T(8,128)(2,1)} %stack.8), calls=%async_computation.6 | async-start | bytes 2097152 | tf_op jit(solution)/shard_map/all_to_all | solution.py:138
  379.7 1.4 copy-start.1
  (3 other events, 3.4 us)
Sparse Core Ops, SparseCore 0:
  141.7 21.2 reduce-scatter.4
  245.4 24.1 reduce-scatter.6
  344.1 23.9 reduce-scatter.8
  372.9 217.9 reduce-scatter.10
